TPU v7x, 32 devices: a whole 2x2x4 slice. The times are simulated.
32 devices in a mesh: section: 4 (over y, core), expert: 4 (over z), mp: 2 (over x).
Axes of the slice: x: 2, y: 2, z: 4, core: 2. Of those that a mesh axis runs over, the one named last changes fastest.
Arguments:
- grad_top: bfloat16 [4, 64, 4096], P(None, 'expert', 'mp'), may hold values from -6 to 6
- w_down: bfloat16 [4, 4, 4096, 4096], P('section', 'expert', None, 'mp'), may hold values from -0.09375 to 0.09375
- w_up: bfloat16 [4, 4, 4096, 4096], P('section', 'expert', 'mp'), may hold values from -0.125 to 0.125
- saved: bfloat16 [4, 4, 4, 16, 4096], P('section', None, 'expert'), may hold values from -6 to 6
- assign: int32 [4, 4, 4, 4], P('section', None, 'expert'), may hold values from 0 to 3, as said below
- keep: int32 [4, 4], replicated, may hold values 0 or 1
Outputs:
- grads: bfloat16 [4, 4, 64, 4096], P('section', None, 'expert', 'mp')
Inputs may be any that keep to these rules, and one draw needn't show every extreme that they name: Each row assign[l, m, i, :] names every expert exactly 1 times.
All inputs are finite; a program needn't handle non-finite values.
Results may differ from a plain program's by a relative error of at most 0.017.
Values may be sent and summed in bfloat16 or wider, within the bound.
A program may use at most 128 MiB of HBM per device.

v0:
```python
import jax
import jax.numpy as jnp
from jax import lax
from jax.sharding import PartitionSpec as P

PER = 1


def shifted(value, axis, by):
    peers = lax.axis_size(axis)
    pairs = [(i, i + by) for i in range(peers) if 0 <= i + by < peers]
    return lax.ppermute(value, axis, pairs)


def body(grad_top, w_down, w_up, saved, assign, keep):
    n_section = lax.axis_size("section")
    n_expert = lax.axis_size("expert")
    section_index = lax.axis_index("section")
    tiles_dev = assign.shape[-1]
    experts = tiles_dev // PER
    group_size = n_expert // experts
    micro_count = grad_top.shape[0]
    token_rows = grad_top.shape[1]
    width = grad_top.shape[2]
    tile_rows = token_rows // tiles_dev
    slab_rows = PER * tile_rows
    down_projection = w_down[0, 0]
    up_proj = w_up[0, 0]
    stored = saved[0, :, 0]
    routes = assign[0, :, 0]
    rows_e = stored.shape[1]
    results = jnp.zeros((micro_count, token_rows, width), jnp.bfloat16)
    incoming = jnp.zeros((token_rows, width), jnp.bfloat16)
    steps_total = micro_count + n_section - 1
    for turn in range(steps_total):
        raw_index = turn - (n_section - 1) + section_index
        active = (raw_index >= 0) & (raw_index < micro_count)
        micro_index = jnp.clip(raw_index, 0, micro_count - 1)
        top_grad = lax.dynamic_index_in_dim(grad_top, micro_index, 0, keepdims=False)
        current = jnp.where(section_index == n_section - 1, top_grad, incoming)
        route_row = lax.dynamic_index_in_dim(routes, micro_index, 0, keepdims=False)
        onehot = (route_row[:, None] == jnp.arange(experts, dtype=jnp.int32)[None, :]).astype(
            jnp.int32
        )
        before = jnp.cumsum(onehot, axis=0) - onehot
        tile_rank = jnp.sum(before * onehot, axis=1)
        position_index = route_row * PER + tile_rank
        placing = (
            position_index[None, :] == jnp.arange(tiles_dev, dtype=jnp.int32)[:, None]
        ).astype(jnp.bfloat16)
        ordered = jnp.dot(
            placing,
            current.reshape(tiles_dev, tile_rows * width),
            preferred_element_type=jnp.float32,
        ).astype(jnp.bfloat16)
        outgoing = jnp.broadcast_to(
            ordered.reshape(experts, 1, slab_rows, width), (experts, group_size, slab_rows, width)
        )
        outgoing = outgoing.reshape(n_expert, slab_rows, width)
        arrived = lax.all_to_all(
            outgoing, "expert", split_axis=0, concat_axis=0, tiled=True
        ).reshape(rows_e, width)
        partial_value = lax.dot_general(
            arrived, down_projection, (((1,), (1,)), ((), ())), preferred_element_type=jnp.float32
        )
        pre_act = lax.dynamic_index_in_dim(stored, micro_index, 0, keepdims=False)
        expert_share_total = lax.psum_scatter(
            partial_value.astype(jnp.bfloat16), "mp", scatter_dimension=0, tiled=True
        ).astype(jnp.float32)
        share_rows = rows_e // lax.axis_size("mp")
        own_rows = lax.dynamic_slice_in_dim(
            pre_act, lax.axis_index("mp") * share_rows, share_rows, 0
        )
        local_grad = jnp.where(own_rows > 0, expert_share_total, 0.0).astype(jnp.bfloat16)
        hidden_grad = lax.all_gather(local_grad, "mp", axis=0, tiled=True)
        back_part = lax.dot_general(
            hidden_grad, up_proj, (((1,), (1,)), ((), ())), preferred_element_type=jnp.float32
        ).astype(jnp.bfloat16)
        returned = lax.all_to_all(
            back_part.reshape(n_expert, slab_rows, width),
            "expert",
            split_axis=0,
            concat_axis=0,
            tiled=True,
        )
        summed = jnp.sum(
            returned.reshape(experts, group_size, slab_rows, width), axis=1, dtype=jnp.float32
        )
        row_updates = jnp.take(summed, position_index, axis=0).reshape(token_rows, width)
        factor = keep[section_index, micro_index].astype(jnp.float32)
        fresh_grad = (current.astype(jnp.float32) + factor * row_updates).astype(jnp.bfloat16)
        previous = lax.dynamic_index_in_dim(results, micro_index, 0, keepdims=False)
        results = lax.dynamic_update_index_in_dim(
            results, jnp.where(active, fresh_grad, previous), micro_index, 0
        )
        if turn + 1 < steps_total:
            incoming = shifted(fresh_grad, "section", -1)
    return results[None]


def solution(mesh):
    placed = (
        P(None, "expert", "mp"),
        P("section", "expert", None, "mp"),
        P("section", "expert", "mp", None),
        P("section", None, "expert", None, None),
        P("section", None, "expert", None),
        P(),
    )
    return jax.shard_map(
        body,
        mesh=mesh,
        in_specs=placed,
        out_specs=P("section", None, "expert", "mp"),
        check_vma=False,
    )
```

profile of v0, /device:TPU:0, one launch (start us, length us, event | category | flops | bytes accessed | tf_op | source)
XLA Modules:
  0.0 437.5 jit_solution(9176409022689948413)
XLA Ops:
  9.5 6.3 %all-to-all-start = ((bf16[4,4,2048]{2,1,0:T(4,128)(2,1)}), bf16[4,4,2048]{2,1,0:T(4,128)(2,1)S(1)}, u32[]{:S(2)}, u32[]{:S(2)}) async-start(bf16[4,4,2048]{2,1,0:T(4,128)(2,1)} %reshape_reshape.21), calls=%async_computation | async-start | bytes 131072 | tf_op jit(solution)/shard_map/all_to_all | solution.py:60
  16.1 5.4 %all-to-all-done = bf16[4,4,2048]{2,1,0:T(4,128)(2,1)S(1)} async-done(((bf16[4,4,2048]{2,1,0:T(4,128)(2,1)}), bf16[4,4,2048]{2,1,0:T(4,128)(2,1)S(1)}, u32[]{:S(2)}, u32[]{:S(2)}) %all-to-all-start) | async-done | bytes 65568 | tf_op jit(solution)/shard_map/all_to_all | solution.py:60
  21.6 10.9 %fusion.28 = bf16[16,4096]{1,0:T(8,128)(2,1)} fusion(bf16[16,2048]{1,0:T(8,128)(2,1)S(1)} %reshape.258, bf16[1,1,4096,2048]{3,2,1,0:T(8,128)(2,1)} %param.9), kind=kOutput, calls=%fused_computation.42 | convolution fusion | flops 268500992 | bytes 16973824 | tf_op jit(solution)/shard_map/dot_general | solution.py:63
  34.5 6.9 %reduce-scatter.8.cloned.1.call-done = bf16[8,4096]{1,0:T(8,128)(2,1)} async-done(((bf16[16,4096]{1,0:T(8,128)(2,1)}), bf16[8,4096]{1,0:T(8,128)(2,1)}) %reduce-scatter.8.cloned.1.call-update) | async-done | bytes 65552 | tf_op jit(solution)/shard_map/reduce_scatter | solution.py:67
  42.3 4.9 %all_gather.21 = bf16[16,4096]{1,0:T(8,128)(2,1)S(1)} all-gather(bf16[8,4096]{1,0:T(8,128)(2,1)S(1)} %select_convert_fusion.6), channel_id=1, replica_groups=mesh['section'=4,'expert'=4,'mp'=2] {'mp'}, dimensions={0}, use_global_device_ids=true | all-gather | bytes 196608 | tf_op jit(solution)/shard_map/all_gather | solution.py:75
  47.3 10.2 %fusion.49 = bf16[16,2048]{1,0:T(8,128)(2,1)S(1)} fusion(bf16[16,4096]{1,0:T(8,128)(2,1)S(1)} %all_gather.21, bf16[1,1,2048,4096]{3,2,1,0:T(8,128)(2,1)} %param.10), kind=kOutput, calls=%fused_computation.49 | convolution fusion | flops 268468224 | bytes 16973824 | tf_op jit(solution)/shard_map/dot_general | solution.py:76
  58.2 4.6 %all-to-all-start.1 = ((bf16[4,4,2048]{2,1,0:T(4,128)(2,1)}), bf16[4,4,2048]{2,1,0:T(4,128)(2,1)S(1)}, u32[]{:S(2)}, u32[]{:S(2)}) async-start(bf16[4,4,2048]{2,1,0:T(4,128)(2,1)} %reshape.259), calls=%async_computation.2 | async-start | bytes 131072 | tf_op jit(solution)/shard_map/all_to_all | solution.py:79
  62.7 5.7 %all-to-all-done.1 = bf16[4,4,2048]{2,1,0:T(4,128)(2,1)S(1)} async-done(((bf16[4,4,2048]{2,1,0:T(4,128)(2,1)}), bf16[4,4,2048]{2,1,0:T(4,128)(2,1)S(1)}, u32[]{:S(2)}, u32[]{:S(2)}) %all-to-all-start.1) | async-done | bytes 65568 | tf_op jit(solution)/shard_map/all_to_all | solution.py:79
  77.1 5.4 %all-to-all-done.2 = bf16[4,4,2048]{2,1,0:T(4,128)(2,1)S(1)} async-done(((bf16[4,4,2048]{2,1,0:T(4,128)(2,1)}), bf16[4,4,2048]{2,1,0:T(4,128)(2,1)S(1)}, u32[]{:S(2)}, u32[]{:S(2)}) %all-to-all-start.2) | async-done | bytes 65568 | tf_op jit(solution)/shard_map/all_to_all | solution.py:60
  82.5 10.9 %fusion.31 = bf16[16,4096]{1,0:T(8,128)(2,1)} fusion(bf16[16,2048]{1,0:T(8,128)(2,1)S(1)} %reshape.261, bf16[1,1,4096,2048]{3,2,1,0:T(8,128)(2,1)} %param.9), kind=kOutput, calls=%fused_computation.43 | convolution fusion | flops 268500992 | bytes 16973824 | tf_op jit(solution)/shard_map/dot_general | solution.py:63
  93.4 8.6 %reduce-scatter.10.cloned.1.call-done = bf16[8,4096]{1,0:T(8,128)(2,1)} async-done(((bf16[16,4096]{1,0:T(8,128)(2,1)}), bf16[8,4096]{1,0:T(8,128)(2,1)}) %reduce-scatter.10.cloned.1.call-update) | async-done | bytes 65552 | tf_op jit(solution)/shard_map/reduce_scatter | solution.py:67
  102.9 4.9 %all_gather.22 = bf16[16,4096]{1,0:T(8,128)(2,1)S(1)} all-gather(bf16[8,4096]{1,0:T(8,128)(2,1)S(1)} %select_convert_fusion.5), channel_id=1, replica_groups=mesh['section'=4,'expert'=4,'mp'=2] {'mp'}, dimensions={0}, use_global_device_ids=true | all-gather | bytes 196608 | tf_op jit(solution)/shard_map/all_gather | solution.py:75
  107.9 10.2 %fusion.52 = bf16[16,2048]{1,0:T(8,128)(2,1)S(1)} fusion(bf16[16,4096]{1,0:T(8,128)(2,1)S(1)} %all_gather.22, bf16[1,1,2048,4096]{3,2,1,0:T(8,128)(2,1)} %param.10), kind=kOutput, calls=%fused_computation.50 | convolution fusion | flops 268468224 | bytes 16973824 | tf_op jit(solution)/shard_map/dot_general | solution.py:76
  123.3 5.7 %all-to-all-done.3 = bf16[4,4,2048]{2,1,0:T(4,128)(2,1)S(1)} async-done(((bf16[4,4,2048]{2,1,0:T(4,128)(2,1)}), bf16[4,4,2048]{2,1,0:T(4,128)(2,1)S(1)}, u32[]{:S(2)}, u32[]{:S(2)}) %all-to-all-start.3) | async-done | bytes 65568 | tf_op jit(solution)/shard_map/all_to_all | solution.py:79
  137.4 5.6 %all-to-all-done.4 = bf16[4,4,2048]{2,1,0:T(4,128)(2,1)S(1)} async-done(((bf16[4,4,2048]{2,1,0:T(4,128)(2,1)}), bf16[4,4,2048]{2,1,0:T(4,128)(2,1)S(1)}, u32[]{:S(2)}, u32[]{:S(2)}) %all-to-all-start.4) | async-done | bytes 65568 | tf_op jit(solution)/shard_map/all_to_all | solution.py:60
  143.0 10.9 %fusion.34 = bf16[16,4096]{1,0:T(8,128)(2,1)} fusion(bf16[16,2048]{1,0:T(8,128)(2,1)S(1)} %reshape.264, bf16[1,1,4096,2048]{3,2,1,0:T(8,128)(2,1)} %param.9), kind=kOutput, calls=%fused_computation.44 | convolution fusion | flops 268500992 | bytes 16973824 | tf_op jit(solution)/shard_map/dot_general | solution.py:63
  154.8 7.8 %reduce-scatter.12.cloned.1.call-done = bf16[8,4096]{1,0:T(8,128)(2,1)} async-done(((bf16[16,4096]{1,0:T(8,128)(2,1)}), bf16[8,4096]{1,0:T(8,128)(2,1)}) %reduce-scatter.12.cloned.1.call-update) | async-done | bytes 65552 | tf_op jit(solution)/shard_map/reduce_scatter | solution.py:67
  163.5 5.3 %all_gather.23 = bf16[16,4096]{1,0:T(8,128)(2,1)S(1)} all-gather(bf16[8,4096]{1,0:T(8,128)(2,1)S(1)} %select_convert_fusion.4), channel_id=1, replica_groups=mesh['section'=4,'expert'=4,'mp'=2] {'mp'}, dimensions={0}, use_global_device_ids=true | all-gather | bytes 196608 | tf_op jit(solution)/shard_map/all_gather | solution.py:75
  168.8 10.2 %fusion.55 = bf16[16,2048]{1,0:T(8,128)(2,1)S(1)} fusion(bf16[16,4096]{1,0:T(8,128)(2,1)S(1)} %all_gather.23, bf16[1,1,2048,4096]{3,2,1,0:T(8,128)(2,1)} %param.10), kind=kOutput, calls=%fused_computation.51 | convolution fusion | flops 268468224 | bytes 16973824 | tf_op jit(solution)/shard_map/dot_general | solution.py:76
  179.7 4.6 %all-to-all-start.5 = ((bf16[4,4,2048]{2,1,0:T(4,128)(2,1)}), bf16[4,4,2048]{2,1,0:T(4,128)(2,1)S(1)}, u32[]{:S(2)}, u32[]{:S(2)}) async-start(bf16[4,4,2048]{2,1,0:T(4,128)(2,1)} %reshape.265), calls=%async_computation.8 | async-start | bytes 131072 | tf_op jit(solution)/shard_map/all_to_all | solution.py:79
  184.3 5.7 %all-to-all-done.5 = bf16[4,4,2048]{2,1,0:T(4,128)(2,1)S(1)} async-done(((bf16[4,4,2048]{2,1,0:T(4,128)(2,1)}), bf16[4,4,2048]{2,1,0:T(4,128)(2,1)S(1)}, u32[]{:S(2)}, u32[]{:S(2)}) %all-to-all-start.5) | async-done | bytes 65568 | tf_op jit(solution)/shard_map/all_to_all | solution.py:79
  194.4 8.1 %all_to_all.70 = bf16[4,4,2048]{2,1,0:T(4,128)(2,1)S(1)} all-to-all(bf16[4,4,2048]{2,1,0:T(4,128)(2,1)S(1)} %reshape_reshape.24), channel_id=1, replica_groups=mesh['section'=4,'expert'=4,'mp'=2] {'expert'}, dimensions={0} | all-to-all | bytes 131072 | tf_op jit(solution)/shard_map/all_to_all | solution.py:60
  202.5 10.9 %fusion.37 = bf16[16,4096]{1,0:T(8,128)(2,1)} fusion(bf16[16,2048]{1,0:T(8,128)(2,1)S(1)} %reshape.267, bf16[1,1,4096,2048]{3,2,1,0:T(8,128)(2,1)} %param.9), kind=kOutput, calls=%fused_computation.45 | convolution fusion | flops 268500992 | bytes 16973824 | tf_op jit(solution)/shard_map/dot_general | solution.py:63
  214.2 7.9 %reduce-scatter.14.cloned.1.call-done = bf16[8,4096]{1,0:T(8,128)(2,1)} async-done(((bf16[16,4096]{1,0:T(8,128)(2,1)}), bf16[8,4096]{1,0:T(8,128)(2,1)}) %reduce-scatter.14.cloned.1.call-update) | async-done | bytes 65552 | tf_op jit(solution)/shard_map/reduce_scatter | solution.py:67
  222.9 5.1 %all_gather.24 = bf16[16,4096]{1,0:T(8,128)(2,1)S(1)} all-gather(bf16[8,4096]{1,0:T(8,128)(2,1)S(1)} %select_convert_fusion.3), channel_id=1, replica_groups=mesh['section'=4,'expert'=4,'mp'=2] {'mp'}, dimensions={0}, use_global_device_ids=true | all-gather | bytes 196608 | tf_op jit(solution)/shard_map/all_gather | solution.py:75
  228.1 10.2 %fusion.58 = bf16[16,2048]{1,0:T(8,128)(2,1)S(1)} fusion(bf16[16,4096]{1,0:T(8,128)(2,1)S(1)} %all_gather.24, bf16[1,1,2048,4096]{3,2,1,0:T(8,128)(2,1)} %param.10), kind=kOutput, calls=%fused_computation.52 | convolution fusion | flops 268468224 | bytes 16973824 | tf_op jit(solution)/shard_map/dot_general | solution.py:76
  238.9 4.6 %all-to-all-start.7 = ((bf16[4,4,2048]{2,1,0:T(4,128)(2,1)}), bf16[4,4,2048]{2,1,0:T(4,128)(2,1)S(1)}, u32[]{:S(2)}, u32[]{:S(2)}) async-start(bf16[4,4,2048]{2,1,0:T(4,128)(2,1)} %reshape.268), calls=%async_computation.11 | async-start | bytes 131072 | tf_op jit(solution)/shard_map/all_to_all | solution.py:79
  243.5 5.7 %all-to-all-done.7 = bf16[4,4,2048]{2,1,0:T(4,128)(2,1)S(1)} async-done(((bf16[4,4,2048]{2,1,0:T(4,128)(2,1)}), bf16[4,4,2048]{2,1,0:T(4,128)(2,1)S(1)}, u32[]{:S(2)}, u32[]{:S(2)}) %all-to-all-start.7) | async-done | bytes 65568 | tf_op jit(solution)/shard_map/all_to_all | solution.py:79
  257.6 5.6 %all-to-all-done.8 = bf16[4,4,2048]{2,1,0:T(4,128)(2,1)S(1)} async-done(((bf16[4,4,2048]{2,1,0:T(4,128)(2,1)}), bf16[4,4,2048]{2,1,0:T(4,128)(2,1)S(1)}, u32[]{:S(2)}, u32[]{:S(2)}) %all-to-all-start.8) | async-done | bytes 65568 | tf_op jit(solution)/shard_map/all_to_all | solution.py:60
  263.2 10.9 %fusion.40 = bf16[16,4096]{1,0:T(8,128)(2,1)} fusion(bf16[16,2048]{1,0:T(8,128)(2,1)S(1)} %reshape.270, bf16[1,1,4096,2048]{3,2,1,0:T(8,128)(2,1)} %param.9), kind=kOutput, calls=%fused_computation.46 | convolution fusion | flops 268500992 | bytes 16973824 | tf_op jit(solution)/shard_map/dot_general | solution.py:63
  275.0 7.8 %reduce-scatter.16.cloned.1.call-done = bf16[8,4096]{1,0:T(8,128)(2,1)} async-done(((bf16[16,4096]{1,0:T(8,128)(2,1)}), bf16[8,4096]{1,0:T(8,128)(2,1)}) %reduce-scatter.16.cloned.1.call-update) | async-done | bytes 65552 | tf_op jit(solution)/shard_map/reduce_scatter | solution.py:67
  283.7 5.2 %all_gather.25 = bf16[16,4096]{1,0:T(8,128)(2,1)S(1)} all-gather(bf16[8,4096]{1,0:T(8,128)(2,1)S(1)} %select_convert_fusion.2), channel_id=1, replica_groups=mesh['section'=4,'expert'=4,'mp'=2] {'mp'}, dimensions={0}, use_global_device_ids=true | all-gather | bytes 196608 | tf_op jit(solution)/shard_map/all_gather | solution.py:75
  288.8 10.2 %fusion.61 = bf16[16,2048]{1,0:T(8,128)(2,1)S(1)} fusion(bf16[16,4096]{1,0:T(8,128)(2,1)S(1)} %all_gather.25, bf16[1,1,2048,4096]{3,2,1,0:T(8,128)(2,1)} %param.10), kind=kOutput, calls=%fused_computation.53 | convolution fusion | flops 268468224 | bytes 16973824 | tf_op jit(solution)/shard_map/dot_general | solution.py:76
  304.3 5.7 %all-to-all-done.9 = bf16[4,4,2048]{2,1,0:T(4,128)(2,1)S(1)} async-done(((bf16[4,4,2048]{2,1,0:T(4,128)(2,1)}), bf16[4,4,2048]{2,1,0:T(4,128)(2,1)S(1)}, u32[]{:S(2)}, u32[]{:S(2)}) %all-to-all-start.9) | async-done | bytes 65568 | tf_op jit(solution)/shard_map/all_to_all | solution.py:79
  314.4 8.1 %all_to_all.71 = bf16[4,4,2048]{2,1,0:T(4,128)(2,1)S(1)} all-to-all(bf16[4,4,2048]{2,1,0:T(4,128)(2,1)S(1)} %reshape_reshape.26), channel_id=1, replica_groups=mesh['section'=4,'expert'=4,'mp'=2] {'expert'}, dimensions={0} | all-to-all | bytes 131072 | tf_op jit(solution)/shard_map/all_to_all | solution.py:60
  322.5 10.9 %fusion.43 = bf16[16,4096]{1,0:T(8,128)(2,1)} fusion(bf16[16,2048]{1,0:T(8,128)(2,1)S(1)} %reshape.273, bf16[1,1,4096,2048]{3,2,1,0:T(8,128)(2,1)} %param.9), kind=kOutput, calls=%fused_computation.47 | convolution fusion | flops 268500992 | bytes 16973824 | tf_op jit(solution)/shard_map/dot_general | solution.py:63
  334.2 7.8 %reduce-scatter.18.cloned.1.call-done = bf16[8,4096]{1,0:T(8,128)(2,1)} async-done(((bf16[16,4096]{1,0:T(8,128)(2,1)}), bf16[8,4096]{1,0:T(8,128)(2,1)}) %reduce-scatter.18.cloned.1.call-update) | async-done | bytes 65552 | tf_op jit(solution)/shard_map/reduce_scatter | solution.py:67
  342.9 5.2 %all_gather.26 = bf16[16,4096]{1,0:T(8,128)(2,1)S(1)} all-gather(bf16[8,4096]{1,0:T(8,128)(2,1)S(1)} %select_convert_fusion.1), channel_id=1, replica_groups=mesh['section'=4,'expert'=4,'mp'=2] {'mp'}, dimensions={0}, use_global_device_ids=true | all-gather | bytes 196608 | tf_op jit(solution)/shard_map/all_gather | solution.py:75
  348.1 10.2 %fusion.64 = bf16[16,2048]{1,0:T(8,128)(2,1)S(1)} fusion(bf16[16,4096]{1,0:T(8,128)(2,1)S(1)} %all_gather.26, bf16[1,1,2048,4096]{3,2,1,0:T(8,128)(2,1)} %param.10), kind=kOutput, calls=%fused_computation.54 | convolution fusion | flops 268468224 | bytes 16973824 | tf_op jit(solution)/shard_map/dot_general | solution.py:76
  359.0 4.6 %all-to-all-start.11 = ((bf16[4,4,2048]{2,1,0:T(4,128)(2,1)}), bf16[4,4,2048]{2,1,0:T(4,128)(2,1)S(1)}, u32[]{:S(2)}, u32[]{:S(2)}) async-start(bf16[4,4,2048]{2,1,0:T(4,128)(2,1)} %reshape.274), calls=%async_computation.17 | async-start | bytes 131072 | tf_op jit(solution)/shard_map/all_to_all | solution.py:79
  363.6 5.7 %all-to-all-done.11 = bf16[4,4,2048]{2,1,0:T(4,128)(2,1)S(1)} async-done(((bf16[4,4,2048]{2,1,0:T(4,128)(2,1)}), bf16[4,4,2048]{2,1,0:T(4,128)(2,1)S(1)}, u32[]{:S(2)}, u32[]{:S(2)}) %all-to-all-start.11) | async-done | bytes 65568 | tf_op jit(solution)/shard_map/all_to_all | solution.py:79
  373.7 8.1 %all_to_all.72 = bf16[4,4,2048]{2,1,0:T(4,128)(2,1)S(1)} all-to-all(bf16[4,4,2048]{2,1,0:T(4,128)(2,1)S(1)} %reshape_reshape.27), channel_id=1, replica_groups=mesh['section'=4,'expert'=4,'mp'=2] {'expert'}, dimensions={0} | all-to-all | bytes 131072 | tf_op jit(solution)/shard_map/all_to_all | solution.py:60
  381.8 10.9 %fusion.46 = bf16[16,4096]{1,0:T(8,128)(2,1)} fusion(bf16[16,2048]{1,0:T(8,128)(2,1)S(1)} %reshape.276, bf16[1,1,4096,2048]{3,2,1,0:T(8,128)(2,1)} %param.9), kind=kOutput, calls=%fused_computation.48 | convolution fusion | flops 268500992 | bytes 16973824 | tf_op jit(solution)/shard_map/dot_general | solution.py:63
  393.3 8.0 %reduce-scatter.20.cloned.1.call-done = bf16[8,4096]{1,0:T(8,128)(2,1)} async-done(((bf16[16,4096]{1,0:T(8,128)(2,1)}), bf16[8,4096]{1,0:T(8,128)(2,1)}) %reduce-scatter.20.cloned.1.call-update) | async-done | bytes 65552 | tf_op jit(solution)/shard_map/reduce_scatter | solution.py:67
  402.2 5.2 %all_gather.27 = bf16[16,4096]{1,0:T(8,128)(2,1)S(1)} all-gather(bf16[8,4096]{1,0:T(8,128)(2,1)S(1)} %select_convert_fusion), channel_id=1, replica_groups=mesh['section'=4,'expert'=4,'mp'=2] {'mp'}, dimensions={0}, use_global_device_ids=true | all-gather | bytes 196608 | tf_op jit(solution)/shard_map/all_gather | solution.py:75
  407.5 10.2 %fusion.67 = bf16[16,2048]{1,0:T(8,128)(2,1)S(1)} fusion(bf16[16,4096]{1,0:T(8,128)(2,1)S(1)} %all_gather.27, bf16[1,1,2048,4096]{3,2,1,0:T(8,128)(2,1)} %param.10), kind=kOutput, calls=%fused_computation.55 | convolution fusion | flops 268468224 | bytes 16973824 | tf_op jit(solution)/shard_map/dot_general | solution.py:76
  418.3 4.6 %all-to-all-start.13 = ((bf16[4,4,2048]{2,1,0:T(4,128)(2,1)}), bf16[4,4,2048]{2,1,0:T(4,128)(2,1)S(1)}, u32[]{:S(2)}, u32[]{:S(2)}) async-start(bf16[4,4,2048]{2,1,0:T(4,128)(2,1)} %reshape.277), calls=%async_computation.20 | async-start | bytes 131072 | tf_op jit(solution)/shard_map/all_to_all | solution.py:79
  423.7 5.0 %all-to-all-done.13 = bf16[4,4,2048]{2,1,0:T(4,128)(2,1)S(1)} async-done(((bf16[4,4,2048]{2,1,0:T(4,128)(2,1)}), bf16[4,4,2048]{2,1,0:T(4,128)(2,1)S(1)}, u32[]{:S(2)}, u32[]{:S(2)}) %all-to-all-start.13) | async-done | bytes 65568 | tf_op jit(solution)/shard_map/all_to_all | solution.py:79
  (171 shorter events, 65.3 us)
Async XLA Ops:
  6.5 26.0 %copy-start.2 = (s32[4,4]{1,0:T(4,128)S(1)}, s32[4,4]{1,0:T(4,128)}, u32[]{:S(2)}) copy-start(s32[4,4]{1,0:T(4,128)} %param.13) | copy-start | bytes 196
  6.5 34.9 %copy-start.1 = (bf16[1,4,1,16,4096]{4,3,2,1,0:T(8,128)(2,1)S(1)}, bf16[1,4,1,16,4096]{4,3,2,1,0:T(8,128)(2,1)}, u32[]{:S(2)}) copy-start(bf16[1,4,1,16,4096]{4,3,2,1,0:T(8,128)(2,1)} %param.11) | copy-start | bytes 1572868
  9.5 12.1 %all-to-all-start = ((bf16[4,4,2048]{2,1,0:T(4,128)(2,1)}), bf16[4,4,2048]{2,1,0:T(4,128)(2,1)S(1)}, u32[]{:S(2)}, u32[]{:S(2)}) async-start(bf16[4,4,2048]{2,1,0:T(4,128)(2,1)} %reshape_reshape.21), calls=%async_computation | async-start | bytes 131072 | tf_op jit(solution)/shard_map/all_to_all | solution.py:60
  15.8 25.7 %reduce-scatter.8.cloned.1.call-start = ((), (), s32[]{:S(2)}) async-start(), calls=%async_computation.21 | async-start | bytes 196608 | tf_op jit(solution)/shard_map/reduce_scatter | solution.py:67
  21.5 47.8 %copy-start = (bf16[4,16,2048]{2,1,0:T(8,128)(2,1)S(1)}, bf16[4,16,2048]{2,1,0:T(8,128)(2,1)}, u32[]{:S(2)}) copy-start(bf16[4,16,2048]{2,1,0:T(8,128)(2,1)} %param.8) | copy-start | bytes 786436
  58.2 10.3 %all-to-all-start.1 = ((bf16[4,4,2048]{2,1,0:T(4,128)(2,1)}), bf16[4,4,2048]{2,1,0:T(4,128)(2,1)S(1)}, u32[]{:S(2)}, u32[]{:S(2)}) async-start(bf16[4,4,2048]{2,1,0:T(4,128)(2,1)} %reshape.259), calls=%async_computation.2 | async-start | bytes 131072 | tf_op jit(solution)/shard_map/all_to_all | solution.py:79
  69.3 3.1 collective-permute-start
  73.4 9.0 %all-to-all-start.2 = ((bf16[4,4,2048]{2,1,0:T(4,128)(2,1)}), bf16[4,4,2048]{2,1,0:T(4,128)(2,1)S(1)}, u32[]{:S(2)}, u32[]{:S(2)}) async-start(bf16[4,4,2048]{2,1,0:T(4,128)(2,1)} %reshape_reshape.22), calls=%async_computation.3 | async-start | bytes 131072 | tf_op jit(solution)/shard_map/all_to_all | solution.py:60
  76.7 25.3 %reduce-scatter.10.cloned.1.call-start = ((), (), s32[]{:S(2)}) async-start(), calls=%async_computation.22 | async-start | bytes 196608 | tf_op jit(solution)/shard_map/reduce_scatter | solution.py:67
  118.7 10.3 %all-to-all-start.3 = ((bf16[4,4,2048]{2,1,0:T(4,128)(2,1)}), bf16[4,4,2048]{2,1,0:T(4,128)(2,1)S(1)}, u32[]{:S(2)}, u32[]{:S(2)}) async-start(bf16[4,4,2048]{2,1,0:T(4,128)(2,1)} %reshape.262), calls=%async_computation.5 | async-start | bytes 131072 | tf_op jit(solution)/shard_map/all_to_all | solution.py:79
  129.9 3.1 collective-permute-start.1
  134.0 9.0 %all-to-all-start.4 = ((bf16[4,4,2048]{2,1,0:T(4,128)(2,1)}), bf16[4,4,2048]{2,1,0:T(4,128)(2,1)S(1)}, u32[]{:S(2)}, u32[]{:S(2)}) async-start(bf16[4,4,2048]{2,1,0:T(4,128)(2,1)} %reshape_reshape.23), calls=%async_computation.6 | async-start | bytes 131072 | tf_op jit(solution)/shard_map/all_to_all | solution.py:60
  137.3 25.3 %reduce-scatter.12.cloned.1.call-start = ((), (), s32[]{:S(2)}) async-start(), calls=%async_computation.23 | async-start | bytes 196608 | tf_op jit(solution)/shard_map/reduce_scatter | solution.py:67
  179.7 10.4 %all-to-all-start.5 = ((bf16[4,4,2048]{2,1,0:T(4,128)(2,1)}), bf16[4,4,2048]{2,1,0:T(4,128)(2,1)S(1)}, u32[]{:S(2)}, u32[]{:S(2)}) async-start(bf16[4,4,2048]{2,1,0:T(4,128)(2,1)} %reshape.265), calls=%async_computation.8 | async-start | bytes 131072 | tf_op jit(solution)/shard_map/all_to_all | solution.py:79
  184.3 37.8 %reduce-scatter.14.cloned.1.call-start = ((), (), s32[]{:S(2)}) async-start(), calls=%async_computation.24 | async-start | bytes 196608 | tf_op jit(solution)/shard_map/reduce_scatter | solution.py:67
  190.9 3.1 collective-permute-start.2
  238.9 10.4 %all-to-all-start.7 = ((bf16[4,4,2048]{2,1,0:T(4,128)(2,1)}), bf16[4,4,2048]{2,1,0:T(4,128)(2,1)S(1)}, u32[]{:S(2)}, u32[]{:S(2)}) async-start(bf16[4,4,2048]{2,1,0:T(4,128)(2,1)} %reshape.268), calls=%async_computation.11 | async-start | bytes 131072 | tf_op jit(solution)/shard_map/all_to_all | solution.py:79
  250.1 3.1 collective-permute-start.3
  254.2 9.0 %all-to-all-start.8 = ((bf16[4,4,2048]{2,1,0:T(4,128)(2,1)}), bf16[4,4,2048]{2,1,0:T(4,128)(2,1)S(1)}, u32[]{:S(2)}, u32[]{:S(2)}) async-start(bf16[4,4,2048]{2,1,0:T(4,128)(2,1)} %reshape_reshape.25), calls=%async_computation.12 | async-start | bytes 131072 | tf_op jit(solution)/shard_map/all_to_all | solution.py:60
  257.5 25.3 %reduce-scatter.16.cloned.1.call-start = ((), (), s32[]{:S(2)}) async-start(), calls=%async_computation.25 | async-start | bytes 196608 | tf_op jit(solution)/shard_map/reduce_scatter | solution.py:67
  299.7 10.3 %all-to-all-start.9 = ((bf16[4,4,2048]{2,1,0:T(4,128)(2,1)}), bf16[4,4,2048]{2,1,0:T(4,128)(2,1)S(1)}, u32[]{:S(2)}, u32[]{:S(2)}) async-start(bf16[4,4,2048]{2,1,0:T(4,128)(2,1)} %reshape.271), calls=%async_computation.14 | async-start | bytes 131072 | tf_op jit(solution)/shard_map/all_to_all | solution.py:79
  304.3 37.8 %reduce-scatter.18.cloned.1.call-start = ((), (), s32[]{:S(2)}) async-start(), calls=%async_computation.26 | async-start | bytes 196608 | tf_op jit(solution)/shard_map/reduce_scatter | solution.py:67
  310.9 3.1 collective-permute-start.4
  359.0 10.4 %all-to-all-start.11 = ((bf16[4,4,2048]{2,1,0:T(4,128)(2,1)}), bf16[4,4,2048]{2,1,0:T(4,128)(2,1)S(1)}, u32[]{:S(2)}, u32[]{:S(2)}) async-start(bf16[4,4,2048]{2,1,0:T(4,128)(2,1)} %reshape.274), calls=%async_computation.17 | async-start | bytes 131072 | tf_op jit(solution)/shard_map/all_to_all | solution.py:79
  363.6 37.8 %reduce-scatter.20.cloned.1.call-start = ((), (), s32[]{:S(2)}) async-start(), calls=%async_computation.27 | async-start | bytes 196608 | tf_op jit(solution)/shard_map/reduce_scatter | solution.py:67
  370.2 3.1 collective-permute-start.5
  418.3 10.4 %all-to-all-start.13 = ((bf16[4,4,2048]{2,1,0:T(4,128)(2,1)}), bf16[4,4,2048]{2,1,0:T(4,128)(2,1)S(1)}, u32[]{:S(2)}, u32[]{:S(2)}) async-start(bf16[4,4,2048]{2,1,0:T(4,128)(2,1)} %reshape.277), calls=%async_computation.20 | async-start | bytes 131072 | tf_op jit(solution)/shard_map/all_to_all | solution.py:79
Sparse Core Ops, SparseCore 0:
  32.6 8.8 reduce-scatter.7
  93.5 8.5 reduce-scatter.9
  154.0 8.5 reduce-scatter.11
  213.5 8.5 reduce-scatter.13
  274.3 8.5 reduce-scatter.15
  333.5 8.5 reduce-scatter.17
  392.8 8.5 reduce-scatter.19
where the time goes:
time: 446 us; the launch traced here: 437 us
  matrix products  149 us (33%)
  waiting for transfers between devices  127 us (28%)
  blocking collectives  60.3 us (14%)
  starting transfers between devices  56.5 us (13%)
  between operations  19 us (4%)
  local copies, waits for them, and re-layouts  15.4 us (3%)
  other arithmetic  10.7 us (2%)
    dot_general x7, matrix products, body(): lax.dot_general(arrived, down_projection, (((1,), (1,)), ((), ())), prefe...  76.1 us
    dot_general x7, matrix products, body(): lax.dot_general(hidden_grad, up_proj, (((1,), (1,)), ((), ())), preferred...  71.3 us
    reduce_scatter x7, waiting for transfers between devices, body(): lax.psum_scatter(partial_value.astype(jnp.bfloat16), 'mp', scatter_dimens...  54.8 us
    all_to_all x7, waiting for transfers between devices, body(): lax.all_to_all(back_part.reshape(n_expert, slab_rows, width), 'expert', s...  39.4 us
    all_gather x7, blocking collectives, body(): hidden_grad = lax.all_gather(local_grad, 'mp', axis=0, tiled=True)  35.9 us
    all_to_all x7, starting transfers between devices, body(): lax.all_to_all(back_part.reshape(n_expert, slab_rows, width), 'expert', s...  32.2 us
    all_to_all x3, blocking collectives, body(): lax.all_to_all(outgoing, 'expert', split_axis=0, concat_axis=0, tiled=True)  24.3 us
    all_to_all x4, waiting for transfers between devices, body(): lax.all_to_all(outgoing, 'expert', split_axis=0, concat_axis=0, tiled=True)  22 us
  transfers between devices with their start and end apart: 24, of which 24 were waited for; matrix products, arithmetic and copies ran while one was open for 1% of the time, Pallas kernels for 0%

commit v1 on v0

--- a/solution.py
+++ b/solution.py
@@ -1,9 +1,16 @@
+import functools
+
 import jax
 import jax.numpy as jnp
 from jax import lax
+from jax.experimental import pallas as pl
+from jax.experimental.pallas import tpu as pltpu
 from jax.sharding import PartitionSpec as P
 
 PER = 1
+COL_CHUNKS = 2
+FF_CHUNKS = 8
+MESH = pl.DeviceIdType.MESH
 
 
 def shifted(value, axis, by):
@@ -12,7 +19,7 @@
     return lax.ppermute(value, axis, pairs)
 
 
-def body(grad_top, w_down, w_up, saved, assign, keep):
+def looped_body(grad_top, w_down, w_up, saved, assign, keep):
     n_section = lax.axis_size("section")
     n_expert = lax.axis_size("expert")
     section_index = lax.axis_index("section")
@@ -98,6 +105,326 @@
     return results[None]
 
 
+NT = (((1,), (1,)), ((), ()))
+
+
+def dot(a, b, dims=(((1,), (0,)), ((), ()))):
+    return lax.dot_general(a, b, dims, preferred_element_type=jnp.float32)
+
+
+def log2(n):
+    return n.bit_length() - 1
+
+
+def fused_kernel(
+    n_section, n_expert, micro, tile,
+    grad, stored, assign, keep, down_hbm, up_hbm,
+    out,
+    down, up, place, place_next, unplace, route, mask,
+    ordered, arrived, partial, to_mate, from_mate, hidden_grad, back, fresh, handed, home,
+    down_sem, up_sem, place_sems, out_sems, in_sems, mate_send, mate_recv,
+    pass_send, pass_recv, home_send, home_recv,
+):
+    s = lax.axis_index("section")
+    e = lax.axis_index("expert")
+    x = lax.axis_index("mp")
+    slab = micro * tile
+    rows = n_expert * slab
+    nc, _, cols = arrived.shape
+    nf, _, fcols = partial.shape
+    halves, _, fhalf = hidden_grad.shape
+    f_per_half = nf // halves
+    last = n_section - 1
+
+    def block(i):
+        return pl.ds(pl.multiple_of(i * slab, slab), slab)
+
+    def down_copy(k, f):
+        spot = pl.ds(pl.multiple_of(f * fcols, fcols), fcols)
+        return pltpu.make_async_copy(
+            down_hbm.at[0, 0, spot, pl.ds(k * cols, cols)], down.at[k, spot], down_sem.at[k, f]
+        )
+
+    def up_copy(h, k):
+        spot = pl.ds(k * cols, cols)
+        return pltpu.make_async_copy(
+            up_hbm.at[0, 0, spot, pl.ds(h * fhalf, fhalf)], up.at[h, spot], up_sem.at[h, k]
+        )
+
+    for k in range(nc):
+        for f in range(nf):
+            down_copy(k, f).start()
+    for h in range(halves):
+        for k in range(nc):
+            up_copy(h, k).start()
+
+    above = lax.rem(s + 1, n_section)
+    below = lax.rem(s + n_section - 1, n_section)
+    barrier = pltpu.get_barrier_semaphore()
+    pl.semaphore_signal(barrier, inc=1, device_id=(s, e, 1 - x), device_id_type=MESH)
+    for d in range(n_expert):
+        peer = lax.rem(e + d, n_expert)
+        if d:
+            pl.semaphore_signal(barrier, inc=1, device_id=(s, peer, x), device_id_type=MESH)
+        pl.semaphore_signal(barrier, inc=1, device_id=(above, peer, x), device_id_type=MESH)
+        pl.semaphore_signal(barrier, inc=1, device_id=(below, peer, x), device_id_type=MESH)
+
+    def parts(index):
+        return index >> log2(slab), (index >> log2(tile)) & (micro - 1), index & (tile - 1)
+
+    def token_parts(index):
+        return index >> log2(n_expert * tile), (index >> log2(tile)) & (n_expert - 1), index & (tile - 1)
+
+    def placing(shape, token_axis):
+        er, mr, rr = parts(lax.broadcasted_iota(jnp.int32, shape, 1 - token_axis))
+        mt, tt, rt = token_parts(lax.broadcasted_iota(jnp.int32, shape, token_axis))
+        chosen = jnp.zeros(shape, jnp.int32)
+        for m in range(micro):
+            for t in range(n_expert):
+                chosen = jnp.where((mt == m) & (tt == t), assign[0, m, 0, t], chosen)
+        hit = (chosen == er) & (mt == mr) & (rt == rr)
+        return jnp.where(hit, 1.0, 0.0).astype(jnp.bfloat16)
+
+    wide = place.shape
+    place[...] = placing(wide, 1)
+    unplace[...] = placing((rows, rows), 0)
+
+    ir, mr, rr = parts(lax.broadcasted_iota(jnp.int32, (rows, rows), 0))
+    mt, it, rt = token_parts(lax.broadcasted_iota(jnp.int32, (rows, rows), 1))
+    swap = jnp.where((ir == it) & (mr == mt) & (rr == rt), 1.0, 0.0).astype(jnp.bfloat16)
+    for f in range(nf):
+        positive = jnp.where(
+            stored[:, f * fcols : (f + 1) * fcols].astype(jnp.float32) > 0, 1.0, 0.0
+        ).astype(jnp.bfloat16)
+        mask[f] = dot(swap, positive).astype(jnp.bfloat16)
+
+    _, row_micro, _ = parts(lax.broadcasted_iota(jnp.int32, (rows, cols), 0))
+    factor = jnp.zeros((rows, cols), jnp.float32)
+    for m in range(micro):
+        factor = jnp.where(row_micro == m, keep[s, m].astype(jnp.float32), factor)
+
+    pl.semaphore_wait(barrier, 3 * n_expert)
+
+    def place_copy():
+        return pltpu.make_async_remote_copy(
+            place, place_next, place_sems.at[0], place_sems.at[1],
+            device_id=(below, e, x), device_id_type=MESH,
+        )
+
+    @pl.when(s > 0)
+    def _():
+        place_copy().start()
+
+    def dispatch_copy(k, d, receiving):
+        peer = lax.rem(e + d, n_expert)
+        slot = peer if receiving else e
+        return pltpu.make_async_remote_copy(
+            ordered.at[k, block(peer)], arrived.at[k, block(slot)],
+            out_sems.at[k, d], in_sems.at[k, slot],
+            device_id=(s, peer, x), device_id_type=MESH,
+        )
+
+    def pass_copy(k, d, receiving):
+        peer = lax.rem(e + d, n_expert)
+        slot = peer if receiving else e
+        return pltpu.make_async_remote_copy(
+            fresh.at[k, block(peer)], handed.at[k, block(slot)],
+            pass_send.at[k, d], pass_recv.at[k, slot],
+            device_id=(below, peer, x), device_id_type=MESH,
+        )
+
+    def home_copy(k, d, receiving):
+        peer = lax.rem(e + d, n_expert)
+        slot = peer if receiving else e
+        return pltpu.make_async_remote_copy(
+            fresh.at[k, block(peer)], home.at[k, block(slot)],
+            home_send.at[k, d], home_recv.at[k, slot],
+            device_id=(s, peer, x), device_id_type=MESH,
+        )
+
+    def mate_copy(f):
+        return pltpu.make_async_remote_copy(
+            to_mate.at[f], from_mate.at[f], mate_send.at[f], mate_recv.at[f],
+            device_id=(s, e, 1 - x), device_id_type=MESH,
+        )
+
+    @pl.when(s < last)
+    def _():
+        place_copy().wait_recv()
+        route[...] = dot(place[...], place_next[...], NT).astype(jnp.bfloat16)
+
+    for k in range(nc):
+        @pl.when(s == last)
+        def _():
+            ordered[k] = dot(
+                place[:, :rows], grad[:, k * cols : (k + 1) * cols]
+            ).astype(jnp.bfloat16)
+
+        @pl.when(s < last)
+        def _():
+            for d in range(n_expert):
+                pass_copy(k, d, True).wait_recv()
+            ordered[k] = dot(route[...], handed[k]).astype(jnp.bfloat16)
+
+        for d in range(1, n_expert):
+            dispatch_copy(k, d, False).start()
+        arrived[k, block(e)] = ordered[k, block(e)]
+
+    for k in range(nc):
+        for d in range(1, n_expert):
+            dispatch_copy(k, d, True).wait_recv()
+
+        @pl.loop(0, nf)
+        def _(f):
+            down_copy(k, f).wait()
+            spot = pl.ds(pl.multiple_of(f * fcols, fcols), fcols)
+            value = dot(arrived[k], down[k, spot], NT)
+            if k:
+                value = value + partial[f]
+            partial[f] = value
+            if k == nc - 1:
+                to_mate[f] = value.astype(jnp.bfloat16)
+                mate_copy(f).start()
+
+    for h in range(halves):
+        for q in range(f_per_half):
+            f = h * f_per_half + q
+            mate_copy(f).wait_recv()
+            total = partial[f] + from_mate[f].astype(jnp.float32)
+            hidden_grad[h, :, q * fcols : (q + 1) * fcols] = jnp.where(
+                mask[f].astype(jnp.float32) > 0, total, 0.0
+            ).astype(jnp.bfloat16)
+        for k in range(nc):
+            up_copy(h, k).wait()
+            value = dot(hidden_grad[h], up[h, k * cols : (k + 1) * cols], NT)
+            if h:
+                value = value + back[k]
+            if h < halves - 1:
+                back[k] = value
+            else:
+                part = value.astype(jnp.bfloat16).astype(jnp.float32)
+                fresh[k] = (arrived[k].astype(jnp.float32) + factor * part).astype(jnp.bfloat16)
+
+                @pl.when(s > 0)
+                def _():
+                    for d in range(n_expert):
+                        pass_copy(k, d, False).start()
+
+                for d in range(1, n_expert):
+                    home_copy(k, d, False).start()
+                home[k, block(e)] = fresh[k, block(e)]
+
+    for k in range(nc):
+        for d in range(1, n_expert):
+            home_copy(k, d, True).wait_recv()
+        out[:, k * cols : (k + 1) * cols] = dot(unplace[...], home[k]).astype(jnp.bfloat16)
+
+    for f in range(nf):
+        mate_copy(f).wait_send()
+    for k in range(nc):
+        for d in range(1, n_expert):
+            dispatch_copy(k, d, False).wait_send()
+            home_copy(k, d, False).wait_send()
+
+    @pl.when(s > 0)
+    def _():
+        place_copy().wait_send()
+        for k in range(nc):
+            for d in range(n_expert):
+                pass_copy(k, d, False).wait_send()
+
+
+def fused_body(mesh_shape, grad_top, w_down, w_up, saved, assign, keep):
+    n_section, n_expert = mesh_shape["section"], mesh_shape["expert"]
+    micro, token_rows, width = grad_top.shape
+    hidden = w_down.shape[2]
+    tile = token_rows // n_expert
+    rows = micro * token_rows
+    cols, fcols, halves = width // COL_CHUNKS, hidden // FF_CHUNKS, 2
+    nc, nf = COL_CHUNKS, FF_CHUNKS
+    bf16, f32 = jnp.bfloat16, jnp.float32
+    dma = pltpu.SemaphoreType.DMA
+    vmem = pl.BlockSpec(memory_space=pltpu.VMEM)
+    smem = pl.BlockSpec(memory_space=pltpu.SMEM)
+    anyspace = pl.BlockSpec(memory_space=pl.ANY)
+    wide = max(rows, 128)
+    result = pl.pallas_call(
+        functools.partial(fused_kernel, n_section, n_expert, micro, tile),
+        out_shape=jax.ShapeDtypeStruct((rows, width), bf16),
+        in_specs=[vmem, vmem, smem, smem, anyspace, anyspace],
+        out_specs=vmem,
+        scratch_shapes=[
+            pltpu.VMEM((nc, hidden, cols), bf16),
+            pltpu.VMEM((halves, width, hidden // halves), bf16),
+            pltpu.VMEM((rows, wide), bf16),
+            pltpu.VMEM((rows, wide), bf16),
+            pltpu.VMEM((rows, rows), bf16),
+            pltpu.VMEM((rows, rows), bf16),
+            pltpu.VMEM((nf, rows, fcols), bf16),
+            pltpu.VMEM((nc, rows, cols), bf16),
+            pltpu.VMEM((nc, rows, cols), bf16),
+            pltpu.VMEM((nf, rows, fcols), f32),
+            pltpu.VMEM((nf, rows, fcols), bf16),
+            pltpu.VMEM((nf, rows, fcols), bf16),
+            pltpu.VMEM((halves, rows, hidden // halves), bf16),
+            pltpu.VMEM((nc, rows, cols), f32),
+            pltpu.VMEM((nc, rows, cols), bf16),
+            pltpu.VMEM((nc, rows, cols), bf16),
+            pltpu.VMEM((nc, rows, cols), bf16),
+            dma((nc, nf)),
+            dma((halves, nc)),
+            dma((2,)),
+            dma((nc, n_expert)),
+            dma((nc, n_expert)),
+            dma((nf,)),
+            dma((nf,)),
+            dma((nc, n_expert)),
+            dma((nc, n_expert)),
+            dma((nc, n_expert)),
+            dma((nc, n_expert)),
+        ],
+        compiler_params=pltpu.CompilerParams(
+            collective_id=0, has_side_effects=True, vmem_limit_bytes=52 * 1024 * 1024
+        ),
+    )(
+        grad_top.reshape(rows, width),
+        saved.reshape(rows, hidden),
+        assign,
+        keep,
+        w_down,
+        w_up,
+    )
+    return result.reshape(1, micro, token_rows, width)
+
+
+def power_of_two(n):
+    return n & (n - 1) == 0
+
+
+def body(mesh_shape, grad_top, w_down, w_up, saved, assign, keep):
+    n_section, n_expert = mesh_shape["section"], mesh_shape["expert"]
+    micro, token_rows, width = grad_top.shape
+    hidden = w_down.shape[2]
+    tiles = assign.shape[-1]
+    weights = 2 * (w_down.size + w_up.size)
+    fits = (
+        PER == 1
+        and tiles == n_expert
+        and mesh_shape["mp"] == 2
+        and n_section >= 3
+        and power_of_two(micro)
+        and power_of_two(n_expert)
+        and power_of_two(token_rows // tiles)
+        and (micro * token_rows // tiles) % 16 == 0
+        and micro * token_rows <= 128
+        and width % (128 * COL_CHUNKS) == 0
+        and hidden % (128 * FF_CHUNKS) == 0
+        and weights <= 33554432
+    )
+    chosen = functools.partial(fused_body, mesh_shape) if fits else looped_body
+    return chosen(grad_top, w_down, w_up, saved, assign, keep)
+
+
 def solution(mesh):
     placed = (
         P(None, "expert", "mp"),
@@ -108,7 +435,7 @@
         P(),
     )
     return jax.shard_map(
-        body,
+        functools.partial(body, mesh.shape),
         mesh=mesh,
         in_specs=placed,
         out_specs=P("section", None, "expert", "mp"),

time: 446 us -> 98.6 us (0.22); the launches traced: 437 us -> 98.4 us
  matrix products: 149 us -> 0 us
  waiting for transfers between devices: 127 us -> 0 us
  Pallas kernels: 0 us -> 94.3 us
  blocking collectives: 60.3 us -> 0 us
  starting transfers between devices: 56.5 us -> 0 us
  between operations: 19 us -> 0.01 us
  local copies, waits for them, and re-layouts: 15.4 us -> 4.06 us
  other arithmetic: 10.7 us -> 0 us
    dot_general x21 -> x0, matrix products: 149 us -> none  [the longest x7 76.1 us: body(): lax.dot_general(arrived, down_projection, (((1,), (1,)), ((), ())), prefe...]
    pallas_call x0 -> x1, Pallas kernels: none -> 94.3 us  [fused_body(): pl.pallas_call(functools.partial(fused_kernel, n_section, n_expert, micro...]
    all_to_all x11 -> x0, waiting for transfers between devices: 61.4 us -> none  [the longest x7 39.4 us: body(): lax.all_to_all(back_part.reshape(n_expert, slab_rows, width), 'expert', s...]
    reduce_scatter x7 -> x0, waiting for transfers between devices: 54.8 us -> none  [body(): lax.psum_scatter(partial_value.astype(jnp.bfloat16), 'mp', scatter_dimens...]
    all_to_all x11 -> x0, starting transfers between devices: 48.4 us -> none  [the longest x7 32.2 us: body(): lax.all_to_all(back_part.reshape(n_expert, slab_rows, width), 'expert', s...]
    all_gather x7 -> x0, blocking collectives: 35.9 us -> none  [body(): hidden_grad = lax.all_gather(local_grad, 'mp', axis=0, tiled=True)]
    all_to_all x3 -> x0, blocking collectives: 24.3 us -> none  [body(): lax.all_to_all(outgoing, 'expert', split_axis=0, concat_axis=0, tiled=True)]
    ppermute x6 -> x0, waiting for transfers between devices: 10.8 us -> none  [shifted(): return lax.ppermute(value, axis, pairs)]
  transfers between devices with their start and end apart: 24 -> 0, of which waited for: 24 -> 0; matrix products, arithmetic and copies ran while one was open for 1% -> 0% of each run, Pallas kernels for 0% -> 0%
where the time goes in v1:
time: 98.6 us; the launch traced here: 98.4 us
  Pallas kernels  94.3 us (96%)
  local copies, waits for them, and re-layouts  4.06 us (4%)
    pallas_call x1, Pallas kernels, fused_body(): pl.pallas_call(functools.partial(fused_kernel, n_section, n_expert, micro...  94.3 us
    unnamed x9, local copies, waits for them, and re-layouts  4.06 us

profile of v1, /device:TPU:0, one launch (start us, length us, event | category | flops | bytes accessed | tf_op | source)
XLA Modules:
  0.0 98.4 jit_solution(832145464900772859)
XLA Ops:
  0.0 0.0 copy-start
  0.0 1.0 %copy-done = bf16[1,4,1,16,4096]{4,3,2,1,0:T(8,128)(2,1)S(1)} copy-done((bf16[1,4,1,16,4096]{4,3,2,1,0:T(8,128)(2,1)S(1)}, bf16[1,4,1,16,4096]{4,3,2,1,0:T(8,128)(2,1)}, u32[]{:S(2)}) %copy-start) | copy-done | bytes 524312
  1.0 0.0 copy-start.1
  1.0 0.9 copy-done.1
  2.0 0.0 copy-start.2
  2.0 0.7 copy-done.2
  2.7 0.0 copy-start.3
  2.7 0.7 copy-done.3
  3.4 94.3 %shard_map.64 = bf16[64,2048]{1,0:T(8,128)(2,1)S(1)} custom-call(bf16[64,2048]{1,0:T(8,128)(2,1)S(1)} %bitcast.5, bf16[64,4096]{1,0:T(8,128)(2,1)S(1)} %bitcast.4, s32[1,4,1,4]{3,2,1,0:T(1,128)S(1)} %copy-done.2, s32[4,4]{1,0:T(4,128)S(1)} %copy-done.3, bf16[1,1,4096,2048]{3,2,1,0:T(8,128)(2,1)} %down_hbm.1, bf16[1,1,2048,4096]{3,2,1,0:T(8,128)(2,1)} %up_hbm.1), custom_call_target="tpu_custom_call" | custom-call | tf_op jit(solution)/shard_map/pallas_call | solution.py:351
  97.7 0.7 copy.8
Async XLA Ops:
  0.0 1.0 %copy-start = (bf16[1,4,1,16,4096]{4,3,2,1,0:T(8,128)(2,1)S(1)}, bf16[1,4,1,16,4096]{4,3,2,1,0:T(8,128)(2,1)}, u32[]{:S(2)}) copy-start(bf16[1,4,1,16,4096]{4,3,2,1,0:T(8,128)(2,1)} %param.9) | copy-start | bytes 1572868
  1.0 0.9 copy-start.1
  2.0 0.7 copy-start.2
  2.7 0.7 copy-start.3

commit v2 on v0

--- a/solution.py
+++ b/solution.py
@@ -1,9 +1,19 @@
+import functools
+
 import jax
 import jax.numpy as jnp
 from jax import lax
+from jax.experimental import pallas as pl
+from jax.experimental.pallas import tpu as pltpu
 from jax.sharding import PartitionSpec as P
 
 PER = 1
+GROUPS = 1
+COL_CHUNKS = 2
+FF_CHUNKS = 8
+FF_HALVES = 2
+VMEM_BYTES = 63 * 1024 * 1024
+MESH = pl.DeviceIdType.MESH
 
 
 def shifted(value, axis, by):
@@ -12,7 +22,7 @@
     return lax.ppermute(value, axis, pairs)
 
 
-def body(grad_top, w_down, w_up, saved, assign, keep):
+def looped_body(grad_top, w_down, w_up, saved, assign, keep):
     n_section = lax.axis_size("section")
     n_expert = lax.axis_size("expert")
     section_index = lax.axis_index("section")
@@ -98,6 +108,404 @@
     return results[None]
 
 
+NT = (((1,), (1,)), ((), ()))
+
+
+def dot(a, b, dims=(((1,), (0,)), ((), ()))):
+    return lax.dot_general(a, b, dims, preferred_element_type=jnp.float32)
+
+
+def log2(n):
+    return n.bit_length() - 1
+
+
+def fused_kernel(
+    n_section, n_expert, micro, tile,
+    grad_hbm, stored_hbm, assign_hbm, keep_hbm, down_hbm, up_hbm,
+    out,
+    grad, stored, assign, keep,
+    down, up, place, place_next, unplace, route, mask,
+    ordered, arrived, partial, to_mate, from_mate, hidden_grad, back, fresh, handed, home,
+    load_sem, down_sem, up_sem, place_sems, out_sems, in_sems, mate_send, mate_recv,
+    pass_send, pass_recv, home_send, home_recv, lift_sems,
+):
+    s = lax.axis_index("section")
+    e = lax.axis_index("expert")
+    x = lax.axis_index("mp")
+    groups, nc, rows, cols = arrived.shape
+    per = micro // groups
+    slab = per * tile
+    _, nf, _, fcols = partial.shape
+    _, halves, _, fhalf = hidden_grad.shape
+    f_per_half = nf // halves
+    last = n_section - 1
+
+    def block(i):
+        return pl.ds(pl.multiple_of(i * slab, slab), slab)
+
+    def loads():
+        pairs = ((assign_hbm, assign), (keep_hbm, keep), (grad_hbm, grad), (stored_hbm, stored))
+        return [
+            pltpu.make_async_copy(source, spot, load_sem.at[i])
+            for i, (source, spot) in enumerate(pairs)
+        ]
+
+    def down_copy(k, f):
+        spot = pl.ds(pl.multiple_of(f * fcols, fcols), fcols)
+        return pltpu.make_async_copy(
+            down_hbm.at[0, 0, spot, pl.ds(k * cols, cols)], down.at[k, spot], down_sem.at[k, f]
+        )
+
+    def up_copy(h, k):
+        spot = pl.ds(k * cols, cols)
+        return pltpu.make_async_copy(
+            up_hbm.at[0, 0, spot, pl.ds(h * fhalf, fhalf)], up.at[h, spot], up_sem.at[h, k]
+        )
+
+    above = lax.rem(s + 1, n_section)
+    below = lax.rem(s + n_section - 1, n_section)
+    barrier = pltpu.get_barrier_semaphore()
+    pl.semaphore_signal(barrier, inc=1, device_id=(s, e, 1 - x), device_id_type=MESH)
+    for d in range(n_expert):
+        peer = lax.rem(e + d, n_expert)
+        if d:
+            pl.semaphore_signal(barrier, inc=1, device_id=(s, peer, x), device_id_type=MESH)
+        pl.semaphore_signal(barrier, inc=1, device_id=(above, peer, x), device_id_type=MESH)
+        pl.semaphore_signal(barrier, inc=1, device_id=(below, peer, x), device_id_type=MESH)
+
+    for copy in loads():
+        copy.start()
+    for k in range(nc):
+        for f in range(nf):
+            down_copy(k, f).start()
+    for h in range(halves):
+        for k in range(nc):
+            up_copy(h, k).start()
+
+    def parts(index):
+        return index >> log2(slab), (index >> log2(tile)) & (per - 1), index & (tile - 1)
+
+    def token_parts(index):
+        return index >> log2(n_expert * tile), (index >> log2(tile)) & (n_expert - 1), index & (tile - 1)
+
+    def placing(g, shape, token_axis):
+        er, mr, rr = parts(lax.broadcasted_iota(jnp.int32, shape, 1 - token_axis))
+        mt, tt, rt = token_parts(lax.broadcasted_iota(jnp.int32, shape, token_axis))
+        chosen = jnp.zeros(shape, jnp.int32)
+        for m in range(per):
+            for t in range(n_expert):
+                chosen = jnp.where((mt == m) & (tt == t), assign[0, g * per + m, 0, t], chosen)
+        hit = (chosen == er) & (mt == mr) & (rt == rr)
+        return jnp.where(hit, 1.0, 0.0).astype(jnp.bfloat16)
+
+    def place_copy():
+        return pltpu.make_async_remote_copy(
+            place, place_next, place_sems.at[0], place_sems.at[1],
+            device_id=(below, e, x), device_id_type=MESH,
+        )
+
+    def dispatch_copy(g, k, d, receiving):
+        peer = lax.rem(e + d, n_expert)
+        if d == 0:
+            return pltpu.make_async_copy(
+                ordered.at[g, k, block(e)], arrived.at[g, k, block(e)], out_sems.at[g, k, 0]
+            )
+        slot = peer if receiving else e
+        return pltpu.make_async_remote_copy(
+            ordered.at[g, k, block(peer)], arrived.at[g, k, block(slot)],
+            out_sems.at[g, k, d], in_sems.at[g, k, slot],
+            device_id=(s, peer, x), device_id_type=MESH,
+        )
+
+    def pass_copy(g, k, d, receiving):
+        peer = lax.rem(e + d, n_expert)
+        slot = peer if receiving else e
+        return pltpu.make_async_remote_copy(
+            fresh.at[g, k, block(peer)], handed.at[g, k, block(slot)],
+            pass_send.at[g, k, d], pass_recv.at[g, k, slot],
+            device_id=(below, peer, x), device_id_type=MESH,
+        )
+
+    def home_copy(g, k, d, receiving):
+        peer = lax.rem(e + d, n_expert)
+        if d == 0:
+            return pltpu.make_async_copy(
+                fresh.at[g, k, block(e)], home.at[g, k, block(e)], home_send.at[g, k, 0]
+            )
+        slot = peer if receiving else e
+        return pltpu.make_async_remote_copy(
+            fresh.at[g, k, block(peer)], home.at[g, k, block(slot)],
+            home_send.at[g, k, d], home_recv.at[g, k, slot],
+            device_id=(s, peer, x), device_id_type=MESH,
+        )
+
+    def lift_copy(g, k):
+        return pltpu.make_async_remote_copy(
+            handed.at[g, k], home.at[g, k], lift_sems.at[0, g, k], lift_sems.at[1, g, k],
+            device_id=(above, e, x), device_id_type=MESH,
+        )
+
+    def mate_copy(g, f):
+        return pltpu.make_async_remote_copy(
+            to_mate.at[g, f], from_mate.at[g, f], mate_send.at[g, f], mate_recv.at[g, f],
+            device_id=(s, e, 1 - x), device_id_type=MESH,
+        )
+
+    assign_load, keep_load, grad_load, stored_load = loads()
+    assign_load.wait()
+    keep_load.wait()
+    for g in range(groups):
+        place[g] = placing(g, place.shape[1:], 1)
+        unplace[g] = placing(g, (rows, rows), 0)
+
+    pl.semaphore_wait(barrier, 3 * n_expert)
+
+    @pl.when(s > 0)
+    def _():
+        place_copy().start()
+
+    grad_load.wait()
+
+    @pl.when(s == last)
+    def _():
+        for g in range(groups):
+            for k in range(nc):
+                ordered[g, k] = dot(
+                    place[g, :, :rows],
+                    grad[g * rows : (g + 1) * rows, k * cols : (k + 1) * cols],
+                ).astype(jnp.bfloat16)
+                for d in (*range(1, n_expert), 0):
+                    dispatch_copy(g, k, d, False).start()
+
+    ir, mr, rr = parts(lax.broadcasted_iota(jnp.int32, (rows, rows), 0))
+    mt, it, rt = token_parts(lax.broadcasted_iota(jnp.int32, (rows, rows), 1))
+    swap = jnp.where((ir == it) & (mr == mt) & (rr == rt), 1.0, 0.0).astype(jnp.bfloat16)
+    stored_load.wait()
+    for g in range(groups):
+        for f in range(nf):
+            block_stored = stored[g * rows : (g + 1) * rows, f * fcols : (f + 1) * fcols]
+            positive = jnp.where(block_stored.astype(jnp.float32) > 0, 1.0, 0.0)
+            mask[g, f] = dot(swap, positive.astype(jnp.bfloat16)).astype(jnp.bfloat16)
+
+    _, row_micro, _ = parts(lax.broadcasted_iota(jnp.int32, (rows, cols), 0))
+
+    @pl.when(s < last)
+    def _():
+        place_copy().wait_recv()
+        for g in range(groups):
+            route[g] = dot(place[g], place_next[g], NT).astype(jnp.bfloat16)
+
+    def enter(g):
+        @pl.when(s < last)
+        def _():
+            for k in range(nc):
+                for d in range(n_expert):
+                    pass_copy(g, k, d, True).wait_recv()
+                ordered[g, k] = dot(route[g], handed[g, k]).astype(jnp.bfloat16)
+                for d in (*range(1, n_expert), 0):
+                    dispatch_copy(g, k, d, False).start()
+
+        for k in range(nc):
+            dispatch_copy(g, k, 0, False).wait()
+            for d in range(1, n_expert):
+                dispatch_copy(g, k, d, True).wait_recv()
+            for f in range(nf):
+                if g == 0:
+                    down_copy(k, f).wait()
+                value = dot(arrived[g, k], down[k, f * fcols : (f + 1) * fcols], NT)
+                if k:
+                    value = value + partial[g, f]
+                partial[g, f] = value
+                if k == nc - 1:
+                    to_mate[g, f] = value.astype(jnp.bfloat16)
+                    mate_copy(g, f).start()
+
+        @pl.when(s < last)
+        def _():
+            for k in range(nc):
+                lift_copy(g, k).start()
+
+    def leave(g):
+        factor = jnp.zeros((rows, cols), jnp.float32)
+        for m in range(per):
+            factor = jnp.where(row_micro == m, keep[s, g * per + m].astype(jnp.float32), factor)
+        for h in range(halves):
+            for q in range(f_per_half):
+                f = h * f_per_half + q
+                mate_copy(g, f).wait_recv()
+                total = partial[g, f] + from_mate[g, f].astype(jnp.float32)
+                hidden_grad[g, h, :, q * fcols : (q + 1) * fcols] = jnp.where(
+                    mask[g, f].astype(jnp.float32) > 0, total, 0.0
+                ).astype(jnp.bfloat16)
+            for k in range(nc):
+                if g == 0:
+                    up_copy(h, k).wait()
+                value = dot(hidden_grad[g, h], up[h, k * cols : (k + 1) * cols], NT)
+                if h:
+                    value = value + back[g, k]
+                if h < halves - 1:
+                    back[g, k] = value
+                else:
+                    part = value.astype(jnp.bfloat16).astype(jnp.float32)
+                    fresh[g, k] = (arrived[g, k].astype(jnp.float32) + factor * part).astype(
+                        jnp.bfloat16
+                    )
+
+                    @pl.when(s > 0)
+                    def _():
+                        for d in range(n_expert):
+                            pass_copy(g, k, d, False).start()
+
+                    @pl.when(s == 0)
+                    def _():
+                        for d in (*range(1, n_expert), 0):
+                            home_copy(g, k, d, False).start()
+
+    for g in range(groups):
+        enter(g)
+        leave(g)
+
+    for g in range(groups):
+        for k in range(nc):
+            @pl.when(s == 0)
+            def _():
+                home_copy(g, k, 0, False).wait()
+                for d in range(1, n_expert):
+                    home_copy(g, k, d, True).wait_recv()
+
+            @pl.when(s > 0)
+            def _():
+                lift_copy(g, k).wait_recv()
+
+            out[g * rows : (g + 1) * rows, k * cols : (k + 1) * cols] = dot(
+                unplace[g], home[g, k]
+            ).astype(jnp.bfloat16)
+
+    for g in range(groups):
+        for f in range(nf):
+            mate_copy(g, f).wait_send()
+        for k in range(nc):
+            for d in range(1, n_expert):
+                dispatch_copy(g, k, d, False).wait_send()
+
+            @pl.when(s == 0)
+            def _():
+                for d in range(1, n_expert):
+                    home_copy(g, k, d, False).wait_send()
+
+            @pl.when(s > 0)
+            def _():
+                for d in range(n_expert):
+                    pass_copy(g, k, d, False).wait_send()
+
+            @pl.when(s < last)
+            def _():
+                lift_copy(g, k).wait_send()
+
+    @pl.when(s > 0)
+    def _():
+        place_copy().wait_send()
+
+
+def fused_body(mesh_shape, grad_top, w_down, w_up, saved, assign, keep):
+    n_section, n_expert = mesh_shape["section"], mesh_shape["expert"]
+    micro, token_rows, width = grad_top.shape
+    hidden = w_down.shape[2]
+    tile = token_rows // n_expert
+    groups, nc, nf, halves = GROUPS, COL_CHUNKS, FF_CHUNKS, FF_HALVES
+    total_rows = micro * token_rows
+    rows = total_rows // groups
+    cols, fcols, fhalf = width // nc, hidden // nf, hidden // halves
+    bf16, f32 = jnp.bfloat16, jnp.float32
+    dma = pltpu.SemaphoreType.DMA
+    anyspace = pl.BlockSpec(memory_space=pl.ANY)
+    wide = max(rows, 128)
+    by_column = (groups, nc, rows, cols)
+    by_hidden = (groups, nf, rows, fcols)
+    result = pl.pallas_call(
+        functools.partial(fused_kernel, n_section, n_expert, micro, tile),
+        out_shape=jax.ShapeDtypeStruct((total_rows, width), bf16),
+        in_specs=[anyspace] * 6,
+        out_specs=pl.BlockSpec(memory_space=pltpu.VMEM),
+        scratch_shapes=[
+            pltpu.VMEM((total_rows, width), bf16),
+            pltpu.VMEM((total_rows, hidden), bf16),
+            pltpu.SMEM(assign.shape, jnp.int32),
+            pltpu.SMEM(keep.shape, jnp.int32),
+            pltpu.VMEM((nc, hidden, cols), bf16),
+            pltpu.VMEM((halves, width, fhalf), bf16),
+            pltpu.VMEM((groups, rows, wide), bf16),
+            pltpu.VMEM((groups, rows, wide), bf16),
+            pltpu.VMEM((groups, rows, rows), bf16),
+            pltpu.VMEM((groups, rows, rows), bf16),
+            pltpu.VMEM(by_hidden, bf16),
+            pltpu.VMEM(by_column, bf16),
+            pltpu.VMEM(by_column, bf16),
+            pltpu.VMEM(by_hidden, f32),
+            pltpu.VMEM(by_hidden, bf16),
+            pltpu.VMEM(by_hidden, bf16),
+            pltpu.VMEM((groups, halves, rows, fhalf), bf16),
+            pltpu.VMEM(by_column, f32),
+            pltpu.VMEM(by_column, bf16),
+            pltpu.VMEM(by_column, bf16),
+            pltpu.VMEM(by_column, bf16),
+            dma((4,)),
+            dma((nc, nf)),
+            dma((halves, nc)),
+            dma((2,)),
+            dma((groups, nc, n_expert)),
+            dma((groups, nc, n_expert)),
+            dma((groups, nf)),
+            dma((groups, nf)),
+            dma((groups, nc, n_expert)),
+            dma((groups, nc, n_expert)),
+            dma((groups, nc, n_expert)),
+            dma((groups, nc, n_expert)),
+            dma((2, groups, nc)),
+        ],
+        compiler_params=pltpu.CompilerParams(
+            collective_id=0, has_side_effects=True, vmem_limit_bytes=VMEM_BYTES
+        ),
+    )(
+        grad_top.reshape(total_rows, width),
+        saved.reshape(total_rows, hidden),
+        assign,
+        keep,
+        w_down,
+        w_up,
+    )
+    return result.reshape(1, micro, token_rows, width)
+
+
+def power_of_two(n):
+    return n & (n - 1) == 0
+
+
+def body(mesh_shape, grad_top, w_down, w_up, saved, assign, keep):
+    n_section, n_expert = mesh_shape["section"], mesh_shape["expert"]
+    micro, token_rows, width = grad_top.shape
+    hidden = w_down.shape[2]
+    tiles = assign.shape[-1]
+    weights = 2 * (w_down.size + w_up.size)
+    fits = (
+        PER == 1
+        and tiles == n_expert
+        and mesh_shape["mp"] == 2
+        and n_section >= 3
+        and power_of_two(micro)
+        and micro % GROUPS == 0
+        and power_of_two(n_expert)
+        and power_of_two(token_rows // tiles)
+        and (micro * token_rows // tiles) % (8 * GROUPS) == 0
+        and micro * token_rows <= 128
+        and width % (128 * COL_CHUNKS) == 0
+        and hidden % (128 * FF_CHUNKS) == 0
+        and weights <= 33554432
+    )
+    chosen = functools.partial(fused_body, mesh_shape) if fits else looped_body
+    return chosen(grad_top, w_down, w_up, saved, assign, keep)
+
+
 def solution(mesh):
     placed = (
         P(None, "expert", "mp"),
@@ -108,7 +516,7 @@
         P(),
     )
     return jax.shard_map(
-        body,
+        functools.partial(body, mesh.shape),
         mesh=mesh,
         in_specs=placed,
         out_specs=P("section", None, "expert", "mp"),

time: 446 us -> 95.9 us (0.22); the launches traced: 437 us -> 95.7 us
  matrix products: 149 us -> 0 us
  waiting for transfers between devices: 127 us -> 0 us
  Pallas kernels: 0 us -> 94.1 us
  blocking collectives: 60.3 us -> 0 us
  starting transfers between devices: 56.5 us -> 0 us
  between operations: 19 us -> 0.01 us
  local copies, waits for them, and re-layouts: 15.4 us -> 1.67 us
  other arithmetic: 10.7 us -> 0 us
    dot_general x21 -> x0, matrix products: 149 us -> none  [the longest x7 76.1 us: body(): lax.dot_general(arrived, down_projection, (((1,), (1,)), ((), ())), prefe...]
    pallas_call x0 -> x1, Pallas kernels: none -> 94.1 us  [fused_body(): pl.pallas_call(functools.partial(fused_kernel, n_section, n_expert, micro...]
    all_to_all x11 -> x0, waiting for transfers between devices: 61.4 us -> none  [the longest x7 39.4 us: body(): lax.all_to_all(back_part.reshape(n_expert, slab_rows, width), 'expert', s...]
    reduce_scatter x7 -> x0, waiting for transfers between devices: 54.8 us -> none  [body(): lax.psum_scatter(partial_value.astype(jnp.bfloat16), 'mp', scatter_dimens...]
    all_to_all x11 -> x0, starting transfers between devices: 48.4 us -> none  [the longest x7 32.2 us: body(): lax.all_to_all(back_part.reshape(n_expert, slab_rows, width), 'expert', s...]
    all_gather x7 -> x0, blocking collectives: 35.9 us -> none  [body(): hidden_grad = lax.all_gather(local_grad, 'mp', axis=0, tiled=True)]
    all_to_all x3 -> x0, blocking collectives: 24.3 us -> none  [body(): lax.all_to_all(outgoing, 'expert', split_axis=0, concat_axis=0, tiled=True)]
    ppermute x6 -> x0, waiting for transfers between devices: 10.8 us -> none  [shifted(): return lax.ppermute(value, axis, pairs)]
  transfers between devices with their start and end apart: 24 -> 0, of which waited for: 24 -> 0; matrix products, arithmetic and copies ran while one was open for 1% -> 0% of each run, Pallas kernels for 0% -> 0%
where the time goes in v2:
time: 95.9 us; the launch traced here: 95.7 us
  Pallas kernels  94.1 us (98%)
  local copies, waits for them, and re-layouts  1.67 us (2%)
    pallas_call x1, Pallas kernels, fused_body(): pl.pallas_call(functools.partial(fused_kernel, n_section, n_expert, micro...  94.1 us

profile of v2, /device:TPU:0, one launch (start us, length us, event | category | flops | bytes accessed | tf_op | source)
XLA Modules:
  0.0 95.7 jit_solution(5284886610183997757)
XLA Ops:
  0.0 94.1 %shard_map.64 = bf16[64,2048]{1,0:T(8,128)(2,1)} custom-call(bf16[64,2048]{1,0:T(8,128)(2,1)} %bitcast.5, bf16[64,4096]{1,0:T(8,128)(2,1)} %bitcast.4, s32[1,4,1,4]{3,2,1,0:T(1,128)} %assign_hbm.1, s32[4,4]{1,0:T(4,128)} %keep_hbm.1, bf16[1,1,4096,2048]{3,2,1,0:T(8,128)(2,1)} %down_hbm.1, bf16[1,1,2048,4096]{3,2,1,0:T(8,128)(2,1)} %up_hbm.1), custom_call_target="tpu_custom_call" | custom-call | tf_op jit(solution)/shard_map/pallas_call | solution.py:425
  94.1 1.7 %copy.8 = bf16[1,4,16,2048]{3,2,1,0:T(8,128)(2,1)} copy(bf16[1,4,16,2048]{3,2,1,0:T(8,128)(2,1)} %bitcast.3) | data formatting | bytes 524288
